TPU v7x, 128 devices: a whole 4x4x4 slice. The times are simulated.
128 devices in a mesh: gx: 8 (over x, core), gy: 16 (over z, y).
Axes of the slice: x: 4, y: 4, z: 4, core: 2. Of those that a mesh axis runs over, the one named last changes fastest.
Arguments:
- upstream: bfloat16 [65536, 256], P(('gx', 'gy')), may hold values from -6 to 6
- saved_hilbert: bfloat16 [65536, 256], P(('gx', 'gy')), may hold values from -40 to 40
- saved_morton: bfloat16 [65536, 256], P(('gx', 'gy')), may hold values from -40 to 40
- gains: float32 [2, 256], replicated, may hold values from 0.1 to 1.9
- w_qkv: bfloat16 [2, 256, 768], replicated, may hold values from -4 to 4
- w_out: bfloat16 [2, 256, 256], replicated, may hold values from -0.375 to 0.375
- hilbert_tiles: int32 [512], replicated, may hold values from 0 to 511, as said below
- morton_tiles: int32 [512], replicated, may hold values from 0 to 511, as said below
Outputs:
- input_grad: bfloat16 [65536, 256], P(('gx', 'gy'))
- qkv_weight_grad: float32 [2, 256, 768], P(None, 'gy')
- out_weight_grad: float32 [2, 256, 256], P(None, 'gy')
- gain_grad: float32 [2, 256], P(None, 'gy')
Inputs may be any that keep to these rules, and one draw needn't show every extreme that they name: `hilbert_tiles`: A permutation of the tile numbers. Tile t is stored on device t // 4 and position j lies on device j // 4, devices numbered gx-major; every tile stays at the same gx index; from one device to another go at most 2 tiles, and some pair of devices reaches 2; counts differ between pairs. `morton_tiles`: A permutation of the tile numbers, devices numbered as for hilbert_tiles; every tile stays at the same gy index; from one device to another go at most 2 tiles, and some pair of devices reaches 2; counts differ between pairs.
All inputs are finite; a program needn't handle non-finite values.
Results may differ from a plain program's by a relative error of at most 0.02.
The roundings to bfloat16 on the way count: a program that leaves them out, or rounds other values in their place, can miss the bound.
Values may be sent and summed in bfloat16 or wider, within the bound.
A program may use at most 128 MiB of HBM per device.

v0:
```python
import jax
import jax.numpy as jnp
from jax import lax
from jax.experimental import pallas as pl
from jax.experimental.pallas import tpu as pltpu
from jax.sharding import PartitionSpec as P

F32 = jnp.float32
BF = jnp.bfloat16
MESH = pl.DeviceIdType.MESH
C = 256
HEADS = 16
HD = 16
TILE = 128
PATCH = 256
EPS = 1e-05
SLAB = 1152
N_GROUPS = 27


def nn(a, b):
    return lax.dot_general(a, b, (((1,), (0,)), ((), ())), preferred_element_type=F32)


def nt(a, b):
    return lax.dot_general(a, b, (((1,), (1,)), ((), ())), preferred_element_type=F32)


def masked(value, head, h):
    return jnp.where(head == h, value, jnp.zeros((), BF))


def forward_norm(x_ref, gain, s):
    rows = x_ref.shape[0]
    for r in range(0, rows, TILE):
        at = slice(r, r + TILE)
        x = x_ref[at, :].astype(F32)
        centred = x - jnp.mean(x, -1, keepdims=True)
        inv = lax.rsqrt(jnp.mean(centred * centred, -1, keepdims=True) + EPS)
        normed = centred * inv
        s["normed"][at, :] = normed
        s["inv"][at, :] = jnp.broadcast_to(inv, (TILE, 128))
        s["hidden"][at, :] = (normed * gain).astype(BF)


def forward_rows(wq_ref, s):
    rows = s["hidden"].shape[0]
    qkv = nn(s["hidden"][...], wq_ref[...]).astype(BF)
    s["q"][...] = qkv[:, :C] * jnp.asarray(0.25, BF)
    s["k"][...] = qkv[:, C : 2 * C]
    s["v"][...] = qkv[:, 2 * C :]
    for p in range(rows // PATCH):
        at = slice(p * PATCH, (p + 1) * PATCH)
        s["qT"][p] = s["q"][at, :].T
        s["kT"][p] = s["k"][at, :].T
        s["vT"][p] = s["v"][at, :].T


def forward_heads(p, s):
    at = slice(p * PATCH, (p + 1) * PATCH)
    head = lax.broadcasted_iota(jnp.int32, (PATCH, C), 1) // HD
    for h in range(HEADS):
        score = nn(masked(s["k"][at, :], head, h), s["qT"][p])
        e = jnp.exp(score - jnp.max(score, axis=0, keepdims=True))
        s["P"][p, h] = (e * (1.0 / jnp.sum(e, axis=0, keepdims=True))).astype(BF)
    for h in range(HEADS):
        at_h = slice(h * HD, (h + 1) * HD)
        s["attT"][p, at_h, :] = nn(s["vT"][p, at_h, :], s["P"][p, h]).astype(BF)


def backward_heads(p, s, w):
    at = slice(p * PATCH, (p + 1) * PATCH)
    head = lax.broadcasted_iota(jnp.int32, (PATCH, C), 1) // HD
    for h in range(HEADS):
        pg = nn(masked(s["v"][at, :], head, h), w["doT"][...])
        pr = s["P"][p, h].astype(F32)
        delta = jnp.sum(pr * pg, axis=0, keepdims=True)
        w["ds"][h] = (pr * (pg - delta)).astype(BF)
    for h in range(HEADS):
        at_h = slice(h * HD, (h + 1) * HD)
        ds = w["ds"][h]
        w["dqT"][at_h, :] = (nn(s["kT"][p, at_h, :], ds) * 0.25).astype(BF)
        w["dkT"][at_h, :] = nt(s["qT"][p, at_h, :], ds).astype(BF)
        w["dvT"][at_h, :] = nt(w["doT"][at_h, :], s["P"][p, h]).astype(BF)


def backward_patch(p, grad_ref, gain, wq_ref, wo_ref, put, s, w):
    at = slice(p * PATCH, (p + 1) * PATCH)
    w["doT"][...] = nt(grad_ref[at, :], wo_ref[...]).astype(BF).T
    backward_heads(p, s, w)
    w["qg"][at, :C] = w["dqT"][...].T
    w["qg"][at, C : 2 * C] = w["dkT"][...].T
    w["qg"][at, 2 * C :] = w["dvT"][...].T
    for t in (2 * p, 2 * p + 1):
        rows = slice(t * TILE, (t + 1) * TILE)
        hg = nt(w["qg"][rows, :], wq_ref[...])
        normed = s["normed"][rows, :]
        gg = jnp.sum(hg * normed, axis=0, keepdims=True)
        if t == 0:
            w["gg"][...] = gg
        else:
            w["gg"][...] += gg
        ng = hg * gain
        mean_ng = jnp.mean(ng, -1, keepdims=True)
        mean_nn = jnp.mean(ng * normed, -1, keepdims=True)
        inv = s["inv"][rows, 0:1]
        put(
            t,
            (
                grad_ref[rows, :].astype(F32) + inv * (ng - mean_ng - normed * mean_nn)
            ).astype(BF),
        )


def weight_grads(grad_ref, s, w, slab):
    slab[1, :, 128:384] = (
        nn(s["attT"][0], grad_ref[:PATCH, :]) + nn(s["attT"][1], grad_ref[PATCH:, :])
    ).astype(BF)
    qkv_part = nn(s["hidden"][...].T, w["qg"][...]).astype(BF)
    slab[0] = qkv_part[:, :640]
    slab[1, :, :128] = qkv_part[:, 640:]
    slab[1, :, 384:512] = jnp.broadcast_to(w["gg"][...], (128, C)).T.astype(BF)
    slab[1, :, 512:] = jnp.zeros((C, 128), BF)


BLOCK_SCRATCH = dict(
    normed=((512, C), F32),
    inv=((512, 128), F32),
    hidden=((512, C), BF),
    q=((512, C), BF),
    k=((512, C), BF),
    v=((512, C), BF),
    qT=((2, C, C), BF),
    kT=((2, C, C), BF),
    vT=((2, C, C), BF),
    P=((2, HEADS, C, C), BF),
    attT=((2, C, C), BF),
)
WORK_SCRATCH = dict(
    doT=((C, C), BF),
    ds=((HEADS, C, C), BF),
    dqT=((C, C), BF),
    dkT=((C, C), BF),
    dvT=((C, C), BF),
    qg=((512, 768), BF),
    gg=((1, C), F32),
)
TILES4 = (4, TILE, C)
LINE = (8, 4, 16, 128)
FAR_GX = ((2, 1), (2, 0), (1, 1), (3, 1), (1, 0), (3, 0), (0, 1))
FAR_GY = sorted(
    ((z, y) for z in range(4) for y in range(4) if (z, y) != (0, 0)),
    key=lambda zy: -sum(min(k, 4 - k) for k in zy),
)
PLANE = (16, 4, 16, 128)
LINE_FLAT = (32, 16, 128)
PLANE_FLAT = (64, 16, 128)
HALF = 640
COMM_SCRATCH = dict(
    a0_hold=(LINE_FLAT, BF),
    a1_hold=(LINE_FLAT, BF),
    a0_pack=(LINE, BF),
    a1_pack=(LINE, BF),
    a0_got=(LINE, BF),
    a1_got=(LINE, BF),
    b0_from=(LINE, BF),
    b1_from=(LINE, BF),
    b0_hold=(LINE_FLAT, BF),
    b1_hold=(LINE_FLAT, BF),
    b0_pack=(LINE, BF),
    b1_pack=(LINE, BF),
    b0_got=(LINE, BF),
    b1_got=(LINE, BF),
    c_from=(PLANE, BF),
    c_hold=(PLANE_FLAT, BF),
    c_pack=(PLANE, BF),
    c_got=(PLANE, BF),
    d_from=(PLANE, BF),
    d_hold=(PLANE_FLAT, BF),
    d_pack=(PLANE, BF),
    d_got=(PLANE, BF),
    grad1=((512, C), BF),
    grad0=((512, C), BF),
    slab1=((2, C, HALF), BF),
    slab0=((2, C, HALF), BF),
    pair1=((C, HALF), BF),
    pair0=((C, HALF), BF),
    both1=((C, HALF), BF),
    both0=((C, HALF), BF),
    red1=((15, 16, HALF), BF),
    red0=((15, 16, HALF), BF),
    redx1=((8, 16, HALF), BF),
    redx0=((8, 16, HALF), BF),
    xm=((512, C), BF),
    xh=((512, C), BF),
    gains=((2, C), F32),
    wq=((2, C, 768), BF),
    wo=((2, C, C), BF),
    tab=((8, 128), jnp.int32),
)


class Links:
    def __init__(self, send_sem, recv_sem):
        self.send_sem, self.recv_sem = send_sem, recv_sem
        self.groups, self.sent = 0, []
        g, gy = lax.axis_index("gx"), lax.axis_index("gy")
        self.g, self.gy = g, gy
        self.core = g % 2
        self.line = [
            lax.rem(g // 2 + x, 4) * 2 + (1 - self.core if c else self.core) for x, c in FAR_GX
        ]
        self.plane = [
            lax.rem(gy // 4 + z, 4) * 4 + lax.rem(gy + y, 4) for z, y in FAR_GY
        ]

    def on_gx(self, g):
        return {"gx": g, "gy": self.gy}

    def on_gy(self, gy):
        return {"gx": self.g, "gy": gy}

    def group(self):
        self.groups += 1
        return self.groups - 1

    def send(self, group, src, dst, device):
        pltpu.make_async_remote_copy(
            src_ref=src,
            dst_ref=dst,
            send_sem=self.send_sem.at[group],
            recv_sem=self.recv_sem.at[group],
            device_id=device,
            device_id_type=MESH,
        ).start()

    def arrived(self, group, ref):
        pltpu.make_async_copy(ref, ref, self.recv_sem.at[group]).wait()
        self.sent.append((group, ref))

    def drain(self):
        for group, ref in self.sent:
            pltpu.make_async_copy(ref, ref, self.send_sem.at[group]).wait()
        self.sent = []

    def greet(self):
        barrier = pltpu.get_barrier_semaphore()
        others = [self.on_gy(gy) for gy in self.plane] + [self.on_gx(g) for g in self.line]
        for other in others:
            pl.semaphore_signal(barrier, inc=1, device_id=other, device_id_type=MESH)

    def greeted(self):
        pl.semaphore_wait(pltpu.get_barrier_semaphore(), 22)


class Exchange:
    def __init__(self, links, others, me, device, source, hold, pack, got, code):
        self.links, self.others, self.me, self.device = links, others, me, device
        self.source, self.hold, self.pack, self.got = source, hold, pack, got
        self.code = code
        self.first, self.second = [], []

    def spread(self, lo, hi):
        part = pl.ds(lo, hi - lo)
        group = self.links.group()
        for i in self.others:
            self.links.send(
                group,
                self.source(i, part),
                self.hold.at[pl.ds(self.me * 4 + lo, hi - lo)],
                self.device(i),
            )
        self.first.append((group, self.hold.at[pl.ds(0, len(self.others) * (hi - lo))]))
        self.keep(lo, hi)

    def keep(self, lo, hi):
        for s in range(lo, hi):
            self.hold[self.me * 4 + s] = self.source(self.me, pl.ds(s, 1))[...].reshape(16, 128)

    def gather(self, lo, hi):
        for group, ref in self.first:
            self.links.arrived(group, ref)
        self.first = []
        part = pl.ds(lo, hi - lo)
        group = self.links.group()
        for r, d in enumerate(self.others):
            for s in range(lo, hi):
                self.pack[r, s] = self.hold[self.code(d, s)]
            self.links.send(
                group, self.pack.at[r, part], self.got.at[self.me, part], self.device(d)
            )
        for s in range(lo, hi):
            self.got[self.me, s] = self.hold[self.code(self.me, s)]
        self.second.append((group, self.got.at[pl.ds(0, len(self.others)), part]))

    def finish(self):
        self.links.arrived(*self.second.pop(0))


class Reduction:
    def __init__(self, links, slab, pair, both, red, redx):
        self.links, self.slab, self.pair, self.both = links, slab, pair, both
        self.red, self.redx = red, redx

    def rows(self, gy):
        return pl.ds(pl.multiple_of(gy * 16, 16), 16)

    def partner(self):
        links = self.links
        self.group = links.group()
        links.send(
            self.group,
            self.slab.at[1 - links.core],
            self.pair,
            links.on_gx(links.g + 1 - 2 * links.core),
        )

    def start(self):
        links = self.links
        links.arrived(self.group, self.pair)
        self.both[...] = (
            self.slab[links.core].astype(F32) + self.pair[...].astype(F32)
        ).astype(BF)
        self.group = links.group()
        for r, to in enumerate(links.plane):
            links.send(
                self.group, self.both.at[self.rows(to)], self.red.at[r], links.on_gy(to)
            )

    def middle(self):
        links = self.links
        links.arrived(self.group, self.red)
        total = self.both[self.rows(links.gy), :].astype(F32)
        for r in range(15):
            total = total + self.red[r].astype(F32)
        self.redx[links.g] = total.astype(BF)
        self.group = links.group()
        for to in links.line:
            links.send(
                self.group, self.redx.at[links.g], self.redx.at[links.g], links.on_gx(to)
            )

    def finish(self):
        self.links.arrived(self.group, self.redx.at[pl.ds(0, 7)])


def kernel(mt_in, ht_in, up, xh_in, xm_in, gains_in, wq_in, wo_in, out_d, out_w, *refs):
    mt, ht, tab_s, send_sem, recv_sem, own_sem = refs[-6:]
    n_b, n_w = len(BLOCK_SCRATCH), len(WORK_SCRATCH)
    s1 = dict(zip(BLOCK_SCRATCH, refs[:n_b]))
    s0 = dict(zip(BLOCK_SCRATCH, refs[n_b : 2 * n_b]))
    w = dict(zip(WORK_SCRATCH, refs[2 * n_b :]))
    m = dict(zip(COMM_SCRATCH, refs[2 * n_b + n_w :]))
    links = Links(send_sem, recv_sem)
    links.greet()
    g, gy = links.g, links.gy
    n_own = [0]

    def bring(src, dst):
        copy = pltpu.make_async_copy(src, dst, own_sem.at[n_own[0]])
        n_own[0] += 1
        copy.start()
        return copy

    wq, wo, gains = m["wq"], m["wo"], m["gains"]
    xm_here = bring(xm_in, m["xm"])
    gains_here = bring(gains_in, gains)
    wq1_here = bring(wq_in.at[1], wq.at[1])
    lists = [bring(mt_in, mt), bring(ht_in, ht)]
    halves = (pl.ds(0, 128), pl.ds(128, 128))
    own_here = [
        bring(up.at[pl.ds(0, 4), g, :, lanes], m[name].at[pl.ds(g * 4, 4)])
        for name, lanes in zip(("a0_hold", "a1_hold"), halves)
    ]
    later = [
        bring(xh_in, m["xh"]),
        bring(wq_in.at[0], wq.at[0]),
        bring(wo_in.at[1], wo.at[1]),
        bring(wo_in.at[0], wo.at[0]),
    ]

    def held_on_line(d, s):
        t = mt[(d * 16 + gy) * 4 + s]
        return ((t >> 6) & 7) * 4 + (t & 3)

    def held_on_plane(d, s):
        return ht[g * 64 + d * 4 + s] & 63

    def back_on_line(d, s):
        return tab_s[0, d * 4 + s] & 31

    def back_on_plane(d, s):
        return tab_s[0, 64 + d * 4 + s] & 63

    def bufs(name):
        return m[name + "_hold"], m[name + "_pack"], m[name + "_got"]

    def line_exchange(name, source, code):
        return Exchange(links, links.line, g, links.on_gx, source, *bufs(name), code)

    a = [
        line_exchange(name, lambda i, p, lanes=lanes: up.at[p, i, :, lanes], held_on_line)
        for name, lanes in zip(("a0", "a1"), halves)
    ]
    b = [
        line_exchange(name, lambda i, p, name=name: m[name + "_from"].at[i, p], back_on_line)
        for name in ("b0", "b1")
    ]
    c = Exchange(
        links, links.plane, gy, links.on_gy, lambda i, p: m["c_from"].at[i, p], *bufs("c"), held_on_plane
    )
    d = Exchange(
        links, links.plane, gy, links.on_gy, lambda i, p: m["d_from"].at[i, p], *bufs("d"), back_on_plane
    )
    red1 = Reduction(links, *(m[n + "1"] for n in ("slab", "pair", "both", "red", "redx")))
    red0 = Reduction(links, *(m[n + "0"] for n in ("slab", "pair", "both", "red", "redx")))

    def put_b(t, tile):
        for i in range(8):
            m["b0_from"][i, t] = tile[16 * i : 16 * i + 16, :128]
            m["b1_from"][i, t] = tile[16 * i : 16 * i + 16, 128:]

    def put_d(t, tile):
        for i in range(16):
            lanes = slice(128 * (i % 2), 128 * (i % 2) + 128)
            m["d_from"][i, t] = tile[16 * (i // 2) : 16 * (i // 2) + 16, lanes]

    def take_a(lo, hi):
        for half in a:
            half.finish()
        for s in range(lo, hi):
            for i in range(8):
                r = s * TILE + 16 * i
                m["grad1"][r : r + 16, :128] = m["a0_got"][i, s]
                m["grad1"][r : r + 16, 128:] = m["a1_got"][i, s]

    def b_to_c(lo, hi):
        for half in b:
            half.finish()
        for s in range(lo, hi):
            for i in range(8):
                m["c_from"][2 * i, s] = m["b0_got"][i, s]
                m["c_from"][2 * i + 1, s] = m["b1_got"][i, s]
        c.spread(lo, hi)

    def take_c(lo, hi):
        c.finish()
        for s in range(lo, hi):
            for i in range(16):
                r = s * TILE + 16 * (i // 2)
                lanes = slice(128 * (i % 2), 128 * (i % 2) + 128)
                m["grad0"][r : r + 16, lanes] = m["c_got"][i, s]

    for half in a:
        half.keep = lambda lo, hi: None
    xm_here.wait()
    gains_here.wait()
    gain0, gain1 = gains[0:1, :], gains[1:2, :]
    forward_norm(m["xm"], gain1, s1)
    links.greeted()
    for half in a:
        half.spread(0, 4)
    wq1_here.wait()
    forward_rows(wq.at[1], s1)
    for copy in lists:
        copy.wait()
    back = jnp.zeros((8, 128), jnp.int32)
    lanes = lax.broadcasted_iota(jnp.int32, (8, 128), 1)
    for j in range(32):
        t = mt[((j // 4) * 16 + gy) * 4 + j % 4]
        back = jnp.where(lanes == ((t >> 6) & 7) * 4 + (t & 3), j, back)
    for j in range(64):
        back = jnp.where(lanes == 64 + (ht[g * 64 + j] & 63), j, back)
    m["tab"][...] = back
    tab_here = bring(m["tab"], tab_s)
    forward_heads(0, s1)
    for copy in own_here:
        copy.wait()
    for lo in (0, 2):
        for half in a:
            half.gather(lo, lo + 2)
    forward_heads(1, s1)
    for copy in later:
        copy.wait()
    forward_norm(m["xh"], gain0, s0)
    forward_rows(wq.at[0], s0)
    forward_heads(0, s0)
    tab_here.wait()

    take_a(0, 2)
    backward_patch(0, m["grad1"], gain1, wq.at[1], wo.at[1], put_b, s1, w)
    for half in b:
        half.spread(0, 2)
    take_a(2, 4)
    backward_patch(1, m["grad1"], gain1, wq.at[1], wo.at[1], put_b, s1, w)
    for half in b:
        half.spread(2, 4)
    weight_grads(m["grad1"], s1, w, m["slab1"])
    for lo in (0, 2):
        for half in b:
            half.gather(lo, lo + 2)
    red1.partner()
    b_to_c(0, 2)
    b_to_c(2, 4)
    forward_heads(1, s0)
    c.gather(0, 2)
    c.gather(2, 4)
    take_c(0, 2)
    red1.start()

    backward_patch(0, m["grad0"], gain0, wq.at[0], wo.at[0], put_d, s0, w)
    d.spread(0, 2)
    take_c(2, 4)
    backward_patch(1, m["grad0"], gain0, wq.at[0], wo.at[0], put_d, s0, w)
    d.spread(2, 4)
    weight_grads(m["grad0"], s0, w, m["slab0"])
    red0.partner()
    red1.middle()
    red0.start()
    d.gather(0, 4)
    red1.finish()
    w1_out = bring(m["redx1"], out_w.at[1])
    d.finish()
    d_out = bring(m["d_got"], out_d)
    red0.middle()
    links.drain()
    red0.finish()
    w0_out = bring(m["redx0"], out_w.at[0])
    links.drain()
    for copy in (w1_out, d_out, w0_out):
        copy.wait()


def write_out(d, sums, out, out_q, out_o, out_g):
    for s in range(4):
        for i in range(16):
            r = s * TILE + 16 * (i // 2)
            lanes = slice(128 * (i % 2), 128 * (i % 2) + 128)
            out[r : r + 16, lanes] = d[i, s]
    diagonal = lax.broadcasted_iota(jnp.int32, (16, 128), 0) == lax.broadcasted_iota(
        jnp.int32, (16, 128), 1
    )
    for b in range(2):
        low, high = (
            sum(sums[b, 2 * x + core].astype(F32) for x in range(4)) for core in (0, 1)
        )
        out_q[b, :, :HALF] = low
        out_q[b, :, HALF:] = high[:, :128]
        out_o[b] = high[:, 128:384]
        row = jnp.sum(jnp.where(diagonal, high[:, 384:512], 0.0), axis=0, keepdims=True)
        out_g[b : b + 1, :] = row[:, :16]


def per_device(up, xh, xm, gains, wq, wo, hilbert_tiles, morton_tiles):
    scratch = (
        list(BLOCK_SCRATCH.values()) * 2
        + list(WORK_SCRATCH.values())
        + list(COMM_SCRATCH.values())
    )
    vmem = pl.BlockSpec(memory_space=pltpu.VMEM)
    hbm = pl.BlockSpec(memory_space=pl.ANY)
    d, sums = pl.pallas_call(
        kernel,
        out_shape=(
            jax.ShapeDtypeStruct(PLANE, BF),
            jax.ShapeDtypeStruct((2, 8, 16, HALF), BF),
        ),
        in_specs=[hbm] * 8,
        out_specs=[hbm] * 2,
        scratch_shapes=[pltpu.VMEM(*v) for v in scratch]
        + [
            pltpu.SMEM((512,), jnp.int32),
            pltpu.SMEM((512,), jnp.int32),
            pltpu.SMEM((8, 128), jnp.int32),
        ]
        + [pltpu.SemaphoreType.DMA((N_GROUPS,))] * 2
        + [pltpu.SemaphoreType.DMA((16,))],
        compiler_params=pltpu.CompilerParams(collective_id=0, has_side_effects=True),
        name="blocks",
    )(morton_tiles, hilbert_tiles, up.reshape(4, 8, 16, C), xh, xm, gains, wq, wo)
    return pl.pallas_call(
        write_out,
        out_shape=(
            jax.ShapeDtypeStruct((512, C), BF),
            jax.ShapeDtypeStruct((2, 16, 768), F32),
            jax.ShapeDtypeStruct((2, 16, 256), F32),
            jax.ShapeDtypeStruct((2, 16), F32),
        ),
        in_specs=[vmem] * 2,
        out_specs=[vmem] * 4,
        name="write_out",
    )(d, sums)


def solution(mesh):
    rows = P(("gx", "gy"), None)
    return jax.shard_map(
        per_device,
        mesh=mesh,
        in_specs=(rows, rows, rows, P(), P(), P(), P(), P()),
        out_specs=(rows, P(None, "gy", None), P(None, "gy", None), P(None, "gy")),
        check_vma=False,
    )
```

profile of v0, /device:TPU:1, one launch (start us, length us, event | category | flops | bytes accessed | tf_op | source)
XLA Modules:
  0.0 69.8 jit_solution(13090810398008210117)
XLA Ops:
  0.6 67.3 %blocks.1 = (bf16[16,4,16,128]{3,2,1,0:T(8,128)(2,1)}, bf16[2,8,16,640]{3,2,1,0:T(8,128)(2,1)}) custom-call(s32[512]{0:T(512)} %mt_in.1, s32[512]{0:T(512)} %ht_in.1, bf16[4,8,16,256]{3,2,1,0:T(8,128)(2,1)} %bitcast.1, bf16[512,256]{1,0:T(8,128)(2,1)} %xh_in.1, bf16[512,256]{1,0:T(8,128)(2,1)} %xm_in.1, f32[2,256]{1,0:T(2,128)} %gains_in.1, ...), custom_call_target="tpu_custom_call" | custom-call | tf_op jit(solution)/shard_map/blocks/pallas_call | solution.py:562
  67.9 1.9 %write_out.1 = (bf16[512,256]{1,0:T(8,128)(2,1)}, f32[2,16,768]{2,1,0:T(8,128)}, f32[2,16,256]{2,1,0:T(8,128)}, f32[2,16]{1,0:T(2,128)}) custom-call(bf16[16,4,16,128]{3,2,1,0:T(8,128)(2,1)} %get-tuple-element.6.d, bf16[2,8,16,640]{3,2,1,0:T(8,128)(2,1)} %get-tuple-element.7.sums), custom_call_target="tpu_custom_call" | custom-call | tf_op jit(solution)/shard_map/write_out/pallas_call | solution.py:581
where the time goes:
time: 70.1 us; the launch traced here: 69.8 us
  Pallas kernels  69.1 us (99%)
    pallas_call x1, Pallas kernels, per_device(): pl.pallas_call(kernel, out_shape=(jax.ShapeDtypeStruct(PLANE, BF), jax.Sh...  67.3 us
    pallas_call x1, Pallas kernels, per_device(): pl.pallas_call(write_out, out_shape=(jax.ShapeDtypeStruct((512, C), BF),...  1.85 us

commit v1 on v0

--- a/solution.py
+++ b/solution.py
@@ -451,6 +451,12 @@
                 lanes = slice(128 * (i % 2), 128 * (i % 2) + 128)
                 m["grad0"][r : r + 16, lanes] = m["c_got"][i, s]
 
+    def apart(*work):
+        @pl.when(g >= 0)
+        def _():
+            for piece in work:
+                piece()
+
     for half in a:
         half.keep = lambda lo, hi: None
     xm_here.wait()
@@ -473,18 +479,20 @@
         back = jnp.where(lanes == 64 + (ht[g * 64 + j] & 63), j, back)
     m["tab"][...] = back
     tab_here = bring(m["tab"], tab_s)
-    forward_heads(0, s1)
+    apart(lambda: forward_heads(0, s1), lambda: forward_heads(1, s1))
     for copy in own_here:
         copy.wait()
     for lo in (0, 2):
         for half in a:
             half.gather(lo, lo + 2)
-    forward_heads(1, s1)
     for copy in later:
         copy.wait()
-    forward_norm(m["xh"], gain0, s0)
-    forward_rows(wq.at[0], s0)
-    forward_heads(0, s0)
+    apart(
+        lambda: forward_norm(m["xh"], gain0, s0),
+        lambda: forward_rows(wq.at[0], s0),
+        lambda: forward_heads(0, s0),
+        lambda: forward_heads(1, s0),
+    )
     tab_here.wait()
 
     take_a(0, 2)
@@ -502,7 +510,6 @@
     red1.partner()
     b_to_c(0, 2)
     b_to_c(2, 4)
-    forward_heads(1, s0)
     c.gather(0, 2)
     c.gather(2, 4)
     take_c(0, 2)

time: 70.1 us -> 67.8 us (0.967)
  Pallas kernels: 69.1 us -> 67.1 us
    pallas_call x1, Pallas kernels: 67.3 us -> 65.2 us  [per_device(): pl.pallas_call(kernel, out_shape=(jax.ShapeDtypeStruct(PLANE, BF), jax.Sh...]
where the time goes in v1:
time: 67.8 us; the launch traced here: 67.7 us
  Pallas kernels  67.1 us (99%)
    pallas_call x1, Pallas kernels, per_device(): pl.pallas_call(kernel, out_shape=(jax.ShapeDtypeStruct(PLANE, BF), jax.Sh...  65.2 us
    pallas_call x1, Pallas kernels, per_device(): pl.pallas_call(write_out, out_shape=(jax.ShapeDtypeStruct((512, C), BF),...  1.85 us

profile of v1, /device:TPU:1, one launch (start us, length us, event | category | flops | bytes accessed | tf_op | source)
XLA Modules:
  0.0 67.7 jit_solution(11803396202724722605)
XLA Ops:
  0.6 65.2 %blocks.1 = (bf16[16,4,16,128]{3,2,1,0:T(8,128)(2,1)}, bf16[2,8,16,640]{3,2,1,0:T(8,128)(2,1)}) custom-call(s32[512]{0:T(512)} %mt_in.1, s32[512]{0:T(512)} %ht_in.1, bf16[4,8,16,256]{3,2,1,0:T(8,128)(2,1)} %bitcast.1, bf16[512,256]{1,0:T(8,128)(2,1)} %xh_in.1, bf16[512,256]{1,0:T(8,128)(2,1)} %xm_in.1, f32[2,256]{1,0:T(2,128)} %gains_in.1, ...), custom_call_target="tpu_custom_call" | custom-call | tf_op jit(solution)/shard_map/blocks/pallas_call | solution.py:569
  65.8 1.9 %write_out.1 = (bf16[512,256]{1,0:T(8,128)(2,1)}, f32[2,16,768]{2,1,0:T(8,128)}, f32[2,16,256]{2,1,0:T(8,128)}, f32[2,16]{1,0:T(2,128)}) custom-call(bf16[16,4,16,128]{3,2,1,0:T(8,128)(2,1)} %get-tuple-element.6.d, bf16[2,8,16,640]{3,2,1,0:T(8,128)(2,1)} %get-tuple-element.7.sums), custom_call_target="tpu_custom_call" | custom-call | tf_op jit(solution)/shard_map/write_out/pallas_call | solution.py:588

commit v2 on v1

--- a/solution.py
+++ b/solution.py
@@ -525,11 +525,11 @@
     red1.middle()
     red0.start()
     d.gather(0, 4)
+    red0.middle()
     red1.finish()
     w1_out = bring(m["redx1"], out_w.at[1])
     d.finish()
     d_out = bring(m["d_got"], out_d)
-    red0.middle()
     links.drain()
     red0.finish()
     w0_out = bring(m["redx0"], out_w.at[0])

time: 67.8 us -> 65.3 us (0.963)
  Pallas kernels: 67.1 us -> 64.5 us
    pallas_call x1, Pallas kernels: 65.2 us -> 62.6 us  [per_device(): pl.pallas_call(kernel, out_shape=(jax.ShapeDtypeStruct(PLANE, BF), jax.Sh...]
where the time goes in v2:
time: 65.3 us; the launch traced here: 65.1 us
  Pallas kernels  64.5 us (99%)
    pallas_call x1, Pallas kernels, per_device(): pl.pallas_call(kernel, out_shape=(jax.ShapeDtypeStruct(PLANE, BF), jax.Sh...  62.6 us
    pallas_call x1, Pallas kernels, per_device(): pl.pallas_call(write_out, out_shape=(jax.ShapeDtypeStruct((512, C), BF),...  1.85 us

profile of v2, /device:TPU:1, one launch (start us, length us, event | category | flops | bytes accessed | tf_op | source)
XLA Modules:
  0.0 65.1 jit_solution(17949175669355808427)
XLA Ops:
  0.6 62.6 %blocks.1 = (bf16[16,4,16,128]{3,2,1,0:T(8,128)(2,1)}, bf16[2,8,16,640]{3,2,1,0:T(8,128)(2,1)}) custom-call(s32[512]{0:T(512)} %mt_in.1, s32[512]{0:T(512)} %ht_in.1, bf16[4,8,16,256]{3,2,1,0:T(8,128)(2,1)} %bitcast.1, bf16[512,256]{1,0:T(8,128)(2,1)} %xh_in.1, bf16[512,256]{1,0:T(8,128)(2,1)} %xm_in.1, f32[2,256]{1,0:T(2,128)} %gains_in.1, ...), custom_call_target="tpu_custom_call" | custom-call | tf_op jit(solution)/shard_map/blocks/pallas_call | solution.py:569
  63.3 1.9 %write_out.1 = (bf16[512,256]{1,0:T(8,128)(2,1)}, f32[2,16,768]{2,1,0:T(8,128)}, f32[2,16,256]{2,1,0:T(8,128)}, f32[2,16]{1,0:T(2,128)}) custom-call(bf16[16,4,16,128]{3,2,1,0:T(8,128)(2,1)} %get-tuple-element.6.d, bf16[2,8,16,640]{3,2,1,0:T(8,128)(2,1)} %get-tuple-element.7.sums), custom_call_target="tpu_custom_call" | custom-call | tf_op jit(solution)/shard_map/write_out/pallas_call | solution.py:588
